TPU v7x, 256 devices: a whole 4x4x8 slice. The times are simulated.
256 devices in a mesh: row: 4 (over y), col: 16 (over x, z_hi), rep: 4 (over z_lo, core).
Axes of the slice: x: 4, y: 4, z: 8 (z_hi: 4, z_lo: 2; z = z_hi * 2 + z_lo), core: 2. Of those that a mesh axis runs over, the one named last changes fastest.
Arguments:
- a_weights: bfloat16 [4, 4096, 2048], P('rep', 'row', 'col'), may hold values from 0 to 10000, as said below
- a_flags: int32 [4, 32, 16], P('rep', 'row', 'col'), may hold values 0 or 1
- b_weights: bfloat16 [4, 2048, 32768], P('rep', 'row', 'col'), may hold values from 0 to 10000, as said below
- b_flags: int32 [4, 16, 256], P('rep', 'row', 'col'), may hold values 0 or 1
- out_flags: int32 [32, 256], P('row', ('col', 'rep')), may hold values 0 or 1
Outputs:
- two_hop: bfloat16 [4096, 32768], P('row', ('col', 'rep'))
Inputs may be any that keep to these rules, and one draw needn't show every extreme that they name: `a_weights`: positive edge weights. `b_weights`: positive edge weights.
All inputs are finite; a program needn't handle non-finite values. No bound on the sum of `a_flags` or of `b_flags` or of `out_flags` on one device may be relied on, other than what follows from the above.
Results may differ from a plain program's by a relative error of at most 0.012.
Values may be sent and summed in bfloat16 or wider, within the bound.
No kernel may reach another device: no remote copies, remote signals or barrier semaphores. Data moves between devices by JAX's collectives and lax.ppermute only.
A program may use at most 64 MiB of HBM per device.

v0:
```python
import jax
import jax.numpy as jnp
from jax import lax
from jax.sharding import PartitionSpec as P


def expand(flags, width):
    return jnp.repeat(jnp.repeat(flags, width, axis=-2), width, axis=-1)


def shards(a_weights, a_flags, b_weights, b_flags, out_flags):
    width = a_weights.shape[1] // a_flags.shape[1]
    a_masked = a_weights * expand(a_flags, width).astype(jnp.bfloat16)
    b_masked = b_weights * expand(b_flags, width).astype(jnp.bfloat16)
    deg_a = 1.0 + lax.psum(jnp.sum(a_masked, axis=(0, 2), dtype=jnp.float32), ("col", "rep"))
    walk_local = (a_masked.astype(jnp.float32) / deg_a[None, :, None]).astype(jnp.bfloat16)
    walk_a = lax.all_gather(walk_local, "col", axis=2, tiled=True)
    deg_b = 1.0 + lax.psum(jnp.sum(b_masked, axis=2, dtype=jnp.float32), "col")
    walk_b = (b_masked.astype(jnp.float32) / deg_b[:, :, None]).astype(jnp.bfloat16)
    left_rows = walk_a[0]
    partial_sum = jnp.dot(
        left_rows,
        lax.all_gather(walk_b, "row", axis=1, tiled=True)[0],
        preferred_element_type=jnp.float32,
    )
    summed = lax.psum_scatter(
        partial_sum.astype(jnp.bfloat16), "rep", scatter_dimension=1, tiled=True
    ).astype(jnp.float32)
    factor = jnp.float32(b_weights.shape[2] * lax.axis_size("col"))
    return (factor * summed * expand(out_flags, width).astype(jnp.float32)).astype(jnp.bfloat16)


def solution(mesh):
    return jax.shard_map(
        shards,
        mesh=mesh,
        in_specs=(
            P("rep", "row", "col"),
            P("rep", "row", "col"),
            P("rep", "row", "col"),
            P("rep", "row", "col"),
            P("row", ("col", "rep")),
        ),
        out_specs=P("row", ("col", "rep")),
        check_vma=False,
    )
```

profile of v0, /device:TPU:1, one launch (start us, length us, event | category | flops | bytes accessed | tf_op | source)
XLA Modules:
  0.0 379.0 jit_solution(2328880365797852931)
XLA Ops:
  6.5 0.0 all-gather.3.cloned.1.call-start
  6.5 0.7 convert_bitcast_fusion.1
  7.2 0.1 broadcast_bitcast_fusion
  7.3 1.3 convert_reduce_fusion.1
  8.6 128.0 %psum.14 = f32[1024]{0:T(1024)S(1)} all-reduce(f32[1024]{0:T(1024)S(1)} %convert_reduce_fusion.1), channel_id=1, replica_groups=mesh['row'=4,'col'=16,'rep'=4] {'col','rep'}, use_global_device_ids=true, to_apply=%region_1.0 | all-reduce | flops 1024 | bytes 8192 | tf_op jit(solution)/shard_map/psum | solution.py:15
  136.6 2.0 fusion.10
  138.6 0.0 all-gather.3.cloned.1.call-update
  138.6 0.0 all-gather.5.cloned.1.call-start
  138.7 0.7 convert_bitcast_fusion
  139.4 2.3 broadcast_in_dim.20
  141.7 2.8 convert_element_type.80
  144.5 2.2 convert_reduce_fusion
  146.7 33.6 %psum.15 = f32[1,512]{1,0:T(1,128)S(1)} all-reduce(f32[1,512]{1,0:T(1,128)S(1)} %bitcast.29), channel_id=1, replica_groups=mesh['row'=4,'col'=16,'rep'=4] {'col'}, use_global_device_ids=true, to_apply=%region_3.0 | all-reduce | flops 512 | bytes 4096 | tf_op jit(solution)/shard_map/psum | solution.py:18
  180.3 3.9 %fusion.2 = bf16[1,512,2048]{2,1,0:T(8,128)(2,1)} fusion(f32[512]{0:T(512)S(1)} %bitcast.28, bf16[1,512,2048]{2,1,0:T(8,128)(2,1)} %param.7, bf16[1,512,2048]{2,1,0:T(8,128)(2,1)S(1)} %convert_element_type.80), kind=kLoop, calls=%fused_computation.4 | loop fusion | flops 4194304 | bytes 6293504 | tf_op jit(solution)/shard_map/convert_element_type | solution.py:19
  184.2 0.0 all-gather.5.cloned.1.call-update
  184.2 0.0 reduce-scatter.2.cloned.1.call-start
  184.3 36.4 %all-gather.3.cloned.1.call-done = bf16[1,1024,2048]{2,1,0:T(8,128)(2,1)} async-done(((bf16[1,1024,128]{2,1,0:T(8,128)(2,1)}), bf16[1,1024,2048]{2,1,0:T(8,128)(2,1)}) %all-gather.3.cloned.1.call-update) | async-done | bytes 4194320 | tf_op jit(solution)/shard_map/all_gather | solution.py:17
  220.6 86.0 %all-gather.5.cloned.1.call-done = bf16[1,2048,2048]{2,1,0:T(8,128)(2,1)} async-done(((bf16[1,512,2048]{2,1,0:T(8,128)(2,1)}), bf16[1,2048,2048]{2,1,0:T(8,128)(2,1)}) %all-gather.5.cloned.1.call-update) | async-done | bytes 8388624 | tf_op jit(solution)/shard_map/all_gather | solution.py:23
  306.6 13.8 %fusion.4 = bf16[1024,2048]{1,0:T(8,128)(2,1)} fusion(bf16[1,2048,2048]{2,1,0:T(8,128)(2,1)} %all-gather.5.cloned.1.call-done, bf16[1,1024,2048]{2,1,0:T(8,128)(2,1)} %all-gather.3.cloned.1.call-done), kind=kOutput, calls=%fused_computation.6 | convolution fusion | flops 8592031744 | bytes 16777216 | tf_op jit(solution)/shard_map/dot_general | solution.py:21
  320.4 0.0 copy-start.1
  320.4 0.0 reduce-scatter.2.cloned.1.call-update
  320.4 0.7 copy-done.1
  321.1 0.1 copy.6
  321.2 48.7 %reduce-scatter.2.cloned.1.call-done = bf16[1024,512]{1,0:T(8,128)(2,1)} async-done(((bf16[1024,2048]{1,0:T(8,128)(2,1)}), bf16[1024,512]{1,0:T(8,128)(2,1)}) %reduce-scatter.2.cloned.1.call-update) | async-done | bytes 1048592 | tf_op jit(solution)/shard_map/reduce_scatter | solution.py:26
  369.8 0.0 copy-start
  369.9 1.2 broadcast_in_dim.22
  371.1 0.0 copy-done
  371.1 1.4 fusion.9
  (5 shorter events, 0.1 us)
Async XLA Ops:
  6.5 214.1 %all-gather.3.cloned.1.call-start = ((), (), s32[]{:S(2)}) async-start(), calls=%async_computation.1 | async-start | bytes 4456448 | tf_op jit(solution)/shard_map/all_gather | solution.py:17
  138.6 168.0 %all-gather.5.cloned.1.call-start = ((), (), s32[]{:S(2)}) async-start(), calls=%async_computation.2 | async-start | bytes 10485760 | tf_op jit(solution)/shard_map/all_gather | solution.py:23
  184.2 185.6 %reduce-scatter.2.cloned.1.call-start = ((), (), s32[]{:S(2)}) async-start(), calls=%async_computation.3 | async-start | bytes 5242880 | tf_op jit(solution)/shard_map/reduce_scatter | solution.py:26
  320.4 0.7 copy-start.1
  369.8 1.3 copy-start
Sparse Core Ops, SparseCore 0:
  138.7 81.8 all-gather.2
  222.4 84.1 all-gather.4
  320.6 49.2 reduce-scatter.1
where the time goes:
time: 379 us
  waiting for transfers between devices  171 us (45%)
  blocking collectives  162 us (43%)
  matrix products  13.8 us (4%)
  between operations  13.1 us (3%)
  other arithmetic  12.1 us (3%)
  local copies, waits for them, and re-layouts  7.21 us (2%)
    psum x1, blocking collectives, shards(): lax.psum(jnp.sum(a_masked, axis=(0, 2), dtype=jnp.float32), ('col', 'rep'))  128 us
    all_gather x1, waiting for transfers between devices, shards(): lax.all_gather(walk_b, 'row', axis=1, tiled=True)[0]  86 us
    reduce_scatter x1, waiting for transfers between devices, shards(): lax.psum_scatter(partial_sum.astype(jnp.bfloat16), 'rep', scatter_dimensi...  48.7 us
    all_gather x1, waiting for transfers between devices, shards(): walk_a = lax.all_gather(walk_local, 'col', axis=2, tiled=True)  36.4 us
    psum x1, blocking collectives, shards(): deg_b = 1.0 + lax.psum(jnp.sum(b_masked, axis=2, dtype=jnp.float32), 'col')  33.6 us
    dot_general x1, matrix products, shards(): jnp.dot(left_rows, lax.all_gather(walk_b, 'row', axis=1, tiled=True)[0],...  13.8 us
  transfers between devices with their start and end apart: 3, of which 3 were waited for; matrix products, arithmetic and copies ran while one was open for 3% of the time, Pallas kernels for 0%

commit v1 on v0

--- a/solution.py
+++ b/solution.py
@@ -12,7 +12,13 @@
     width = a_weights.shape[1] // a_flags.shape[1]
     a_masked = a_weights * expand(a_flags, width).astype(jnp.bfloat16)
     b_masked = b_weights * expand(b_flags, width).astype(jnp.bfloat16)
-    deg_a = 1.0 + lax.psum(jnp.sum(a_masked, axis=(0, 2), dtype=jnp.float32), ("col", "rep"))
+
+    def connect_the_ratios(local):
+        for m in ("rep", "col"):
+            local = jax.lax.psum(local, m)
+        return local
+
+    deg_a = 1.0 + connect_the_ratios(jnp.sum(a_masked, axis=(0, 2), dtype=jnp.float32))
     walk_local = (a_masked.astype(jnp.float32) / deg_a[None, :, None]).astype(jnp.bfloat16)
     walk_a = lax.all_gather(walk_local, "col", axis=2, tiled=True)
     deg_b = 1.0 + lax.psum(jnp.sum(b_masked, axis=2, dtype=jnp.float32), "col")

time: 379 us -> 307 us (0.81)
  blocking collectives: 162 us -> 47.4 us
  waiting for transfers between devices: 171 us -> 216 us
    psum x1, blocking collectives: 128 us -> 8.26 us  [connect_the_ratios(): local = jax.lax.psum(local, m)]
    all_gather x1, waiting for transfers between devices: 36.4 us -> 81.2 us  [shards(): walk_a = lax.all_gather(walk_local, 'col', axis=2, tiled=True)]
    psum x1, blocking collectives: 33.6 us -> 39.2 us  [shards(): deg_b = 1.0 + lax.psum(jnp.sum(b_masked, axis=2, dtype=jnp.float32), 'col')]
  transfers between devices with their start and end apart: 3 -> 3, of which waited for: 3 -> 3; matrix products, arithmetic and copies ran while one was open for 3% -> 1% of each run, Pallas kernels for 0% -> 0%
where the time goes in v1:
time: 307 us
  waiting for transfers between devices  216 us (70%)
  blocking collectives  47.4 us (15%)
  matrix products  13.8 us (4%)
  between operations  13.2 us (4%)
  other arithmetic  9.59 us (3%)
  local copies, waits for them, and re-layouts  7.25 us (2%)
    all_gather x1, waiting for transfers between devices, shards(): lax.all_gather(walk_b, 'row', axis=1, tiled=True)[0]  85.8 us
    all_gather x1, waiting for transfers between devices, shards(): walk_a = lax.all_gather(walk_local, 'col', axis=2, tiled=True)  81.2 us
    reduce_scatter x1, waiting for transfers between devices, shards(): lax.psum_scatter(partial_sum.astype(jnp.bfloat16), 'rep', scatter_dimensi...  48.7 us
    psum x1, blocking collectives, shards(): deg_b = 1.0 + lax.psum(jnp.sum(b_masked, axis=2, dtype=jnp.float32), 'col')  39.2 us
    dot_general x1, matrix products, shards(): jnp.dot(left_rows, lax.all_gather(walk_b, 'row', axis=1, tiled=True)[0],...  13.8 us
    psum x1, blocking collectives, connect_the_ratios(): local = jax.lax.psum(local, m)  8.26 us
  transfers between devices with their start and end apart: 3, of which 3 were waited for; matrix products, arithmetic and copies ran while one was open for 1% of the time, Pallas kernels for 0%

profile of v1, /device:TPU:1, one launch (start us, length us, event | category | flops | bytes accessed | tf_op | source)
XLA Modules:
  0.0 307.1 jit_solution(14390262425811864992)
XLA Ops:
  6.5 0.0 all-gather.3.cloned.1.call-start
  6.5 0.7 convert_bitcast_fusion
  7.2 2.3 broadcast_in_dim.20
  9.5 0.0 copy-start.3
  9.5 0.0 copy-start
  9.5 2.9 convert_element_type.80
  12.4 0.0 copy-done.3
  12.4 0.1 broadcast_bitcast_fusion
  12.5 0.0 copy-done
  12.5 0.4 convert_reduce_fusion.1
  12.9 8.3 %psum.21 = f32[1024]{0:T(1024)S(1)} all-reduce(f32[1024]{0:T(1024)S(1)} %convert_reduce_fusion.1), channel_id=1, replica_groups=mesh['row'=4,'col'=16,'rep'=4] {'rep'}, use_global_device_ids=true, to_apply=%region_1.0 | all-reduce | flops 1024 | bytes 8192 | tf_op jit(solution)/shard_map/psum | solution.py:18
  21.1 2.2 convert_reduce_fusion
  23.3 39.2 %all-reduce = (f32[1,512]{1,0:T(1,128)S(1)}, f32[1024]{0:T(1024)S(1)}) all-reduce(f32[1,512]{1,0:T(1,128)S(1)} %bitcast.28, f32[1024]{0:T(1024)S(1)} %psum.21), channel_id=1, replica_groups=mesh['row'=4,'col'=16,'rep'=4] {'col'}, use_global_device_ids=true, to_apply=%region_4.0 | all-reduce | flops 1536 | bytes 12288 | tf_op jit(solution)/shard_map/psum | solution.py:24
  62.5 1.0 fusion.10
  63.6 0.0 all-gather.3.cloned.1.call-update
  63.6 0.0 all-gather.5.cloned.1.call-start
  63.7 3.9 %fusion.2 = bf16[1,512,2048]{2,1,0:T(8,128)(2,1)} fusion(f32[512]{0:T(512)S(1)} %bitcast.29, bf16[1,512,2048]{2,1,0:T(8,128)(2,1)} %param.7, bf16[1,512,2048]{2,1,0:T(8,128)(2,1)S(1)} %convert_element_type.80), kind=kLoop, calls=%fused_computation.4 | loop fusion | flops 4194304 | bytes 6293504 | tf_op jit(solution)/shard_map/convert_element_type | solution.py:25
  67.5 0.0 all-gather.5.cloned.1.call-update
  67.6 0.0 reduce-scatter.2.cloned.1.call-start
  67.6 81.2 %all-gather.3.cloned.1.call-done = bf16[1,1024,2048]{2,1,0:T(8,128)(2,1)} async-done(((bf16[1,1024,128]{2,1,0:T(8,128)(2,1)}), bf16[1,1024,2048]{2,1,0:T(8,128)(2,1)}) %all-gather.3.cloned.1.call-update) | async-done | bytes 4194320 | tf_op jit(solution)/shard_map/all_gather | solution.py:23
  148.8 85.8 %all-gather.5.cloned.1.call-done = bf16[1,2048,2048]{2,1,0:T(8,128)(2,1)} async-done(((bf16[1,512,2048]{2,1,0:T(8,128)(2,1)}), bf16[1,2048,2048]{2,1,0:T(8,128)(2,1)}) %all-gather.5.cloned.1.call-update) | async-done | bytes 8388624 | tf_op jit(solution)/shard_map/all_gather | solution.py:29
  234.6 13.8 %fusion.4 = bf16[1024,2048]{1,0:T(8,128)(2,1)} fusion(bf16[1,2048,2048]{2,1,0:T(8,128)(2,1)} %all-gather.5.cloned.1.call-done, bf16[1,1024,2048]{2,1,0:T(8,128)(2,1)} %all-gather.3.cloned.1.call-done), kind=kOutput, calls=%fused_computation.6 | convolution fusion | flops 8592031744 | bytes 16777216 | tf_op jit(solution)/shard_map/dot_general | solution.py:27
  248.4 0.0 copy-start.2
  248.4 0.0 reduce-scatter.2.cloned.1.call-update
  248.5 0.7 copy-done.2
  249.1 0.1 copy.6
  249.2 48.7 %reduce-scatter.2.cloned.1.call-done = bf16[1024,512]{1,0:T(8,128)(2,1)} async-done(((bf16[1024,2048]{1,0:T(8,128)(2,1)}), bf16[1024,512]{1,0:T(8,128)(2,1)}) %reduce-scatter.2.cloned.1.call-update) | async-done | bytes 1048592 | tf_op jit(solution)/shard_map/reduce_scatter | solution.py:32
  297.9 0.0 copy-start.1
  297.9 1.2 broadcast_in_dim.22
  299.1 0.0 copy-done.1
  299.2 1.4 fusion.9
  (6 shorter events, 0.1 us)
Async XLA Ops:
  6.5 142.3 %all-gather.3.cloned.1.call-start = ((), (), s32[]{:S(2)}) async-start(), calls=%async_computation.1 | async-start | bytes 4456448 | tf_op jit(solution)/shard_map/all_gather | solution.py:23
  9.5 2.9 copy-start.3
  9.5 3.0 copy-start
  63.6 171.0 %all-gather.5.cloned.1.call-start = ((), (), s32[]{:S(2)}) async-start(), calls=%async_computation.2 | async-start | bytes 10485760 | tf_op jit(solution)/shard_map/all_gather | solution.py:29
  67.6 230.3 %reduce-scatter.2.cloned.1.call-start = ((), (), s32[]{:S(2)}) async-start(), calls=%async_computation.3 | async-start | bytes 5242880 | tf_op jit(solution)/shard_map/reduce_scatter | solution.py:32
  248.4 0.7 copy-start.2
  297.9 1.3 copy-start.1
Sparse Core Ops, SparseCore 0:
  63.7 85.0 all-gather.2
  150.6 83.9 all-gather.4
  248.6 49.2 reduce-scatter.1

commit v2 on v0

--- a/solution.py
+++ b/solution.py
@@ -2,6 +2,7 @@
 import jax.numpy as jnp
 from jax import lax
 from jax.sharding import PartitionSpec as P
+from jax.lax import all_to_all, axis_size
 
 
 def expand(flags, width):
@@ -18,10 +19,12 @@
     deg_b = 1.0 + lax.psum(jnp.sum(b_masked, axis=2, dtype=jnp.float32), "col")
     walk_b = (b_masked.astype(jnp.float32) / deg_b[:, :, None]).astype(jnp.bfloat16)
     left_rows = walk_a[0]
+    advance_sectors_on = lambda packet, along_axis: jnp.concatenate(
+        all_to_all(jnp.stack([packet for _ in range(axis_size(along_axis))], 0), along_axis, 0, 0),
+        1,
+    )
     partial_sum = jnp.dot(
-        left_rows,
-        lax.all_gather(walk_b, "row", axis=1, tiled=True)[0],
-        preferred_element_type=jnp.float32,
+        left_rows, advance_sectors_on(walk_b, "row")[0], preferred_element_type=jnp.float32
     )
     summed = lax.psum_scatter(
         partial_sum.astype(jnp.bfloat16), "rep", scatter_dimension=1, tiled=True

time: 379 us -> 350 us (0.923)
  waiting for transfers between devices: 171 us -> 57 us
  blocking collectives: 162 us -> 246 us
    all_gather x1 -> x0, waiting for transfers between devices: 86 us -> none  [shards(): lax.all_gather(walk_b, 'row', axis=1, tiled=True)[0]]
    all_to_all x0 -> x1, blocking collectives: none -> 84.7 us  [shards(): all_to_all(jnp.stack([packet for _ in range(axis_size(along_axis))], 0),...]
    all_gather x1, waiting for transfers between devices: 36.4 us -> 0.01 us  [shards(): walk_a = lax.all_gather(walk_local, 'col', axis=2, tiled=True)]
    reduce_scatter x1, waiting for transfers between devices: 48.7 us -> 56.9 us  [shards(): lax.psum_scatter(partial_sum.astype(jnp.bfloat16), 'rep', scatter_dimensi...]
  transfers between devices with their start and end apart: 3 -> 2, of which waited for: 3 -> 1; matrix products, arithmetic and copies ran while one was open for 3% -> 3% of each run, Pallas kernels for 0% -> 0%
where the time goes in v2:
time: 350 us
  blocking collectives  246 us (70%)
  waiting for transfers between devices  57 us (16%)
  matrix products  13.8 us (4%)
  between operations  13.5 us (4%)
  other arithmetic  10.8 us (3%)
  local copies, waits for them, and re-layouts  8.29 us (2%)
    psum x1, blocking collectives, shards(): lax.psum(jnp.sum(a_masked, axis=(0, 2), dtype=jnp.float32), ('col', 'rep'))  128 us
    all_to_all x1, blocking collectives, shards(): all_to_all(jnp.stack([packet for _ in range(axis_size(along_axis))], 0),...  84.7 us
    reduce_scatter x1, waiting for transfers between devices, shards(): lax.psum_scatter(partial_sum.astype(jnp.bfloat16), 'rep', scatter_dimensi...  56.9 us
    psum x1, blocking collectives, shards(): deg_b = 1.0 + lax.psum(jnp.sum(b_masked, axis=2, dtype=jnp.float32), 'col')  33.6 us
    dot_general x1, matrix products, shards(): jnp.dot(left_rows, advance_sectors_on(walk_b, 'row')[0], preferred_elemen...  13.8 us
  transfers between devices with their start and end apart: 2, of which 1 were waited for; matrix products, arithmetic and copies ran while one was open for 3% of the time, Pallas kernels for 0%

profile of v2, /device:TPU:1, one launch (start us, length us, event | category | flops | bytes accessed | tf_op | source)
XLA Modules:
  0.0 349.7 jit_solution(8260688940077643840)
XLA Ops:
  6.5 0.0 all-gather.2.cloned.1.call-start
  6.5 0.7 convert_bitcast_fusion.1
  7.2 0.1 broadcast_bitcast_fusion
  7.3 1.3 convert_reduce_fusion.1
  8.6 128.0 %psum.14 = f32[1024]{0:T(1024)S(1)} all-reduce(f32[1024]{0:T(1024)S(1)} %convert_reduce_fusion.1), channel_id=1, replica_groups=mesh['row'=4,'col'=16,'rep'=4] {'col','rep'}, use_global_device_ids=true, to_apply=%region_1.0 | all-reduce | flops 1024 | bytes 8192 | tf_op jit(solution)/shard_map/psum | solution.py:16
  136.6 2.0 fusion.8
  138.6 0.0 all-gather.2.cloned.1.call-update
  138.6 0.0 reduce-scatter.2.cloned.1.call-start
  138.7 0.7 convert_bitcast_fusion
  139.4 2.3 broadcast_in_dim.20
  141.7 2.8 convert_element_type.82
  144.5 2.2 convert_reduce_fusion
  146.7 33.6 %psum.15 = f32[1,512]{1,0:T(1,128)S(1)} all-reduce(f32[1,512]{1,0:T(1,128)S(1)} %bitcast.29), channel_id=1, replica_groups=mesh['row'=4,'col'=16,'rep'=4] {'col'}, use_global_device_ids=true, to_apply=%region_3.0 | all-reduce | flops 512 | bytes 4096 | tf_op jit(solution)/shard_map/psum | solution.py:19
  180.3 2.5 fusion.6
  182.8 1.1 stack.2
  183.9 84.7 %all_to_all.5 = bf16[4,1,512,2048]{3,2,1,0:T(8,128)(2,1)} all-to-all(bf16[4,1,512,2048]{3,2,1,0:T(8,128)(2,1)S(1)} %stack.2), channel_id=1, replica_groups=mesh['row'=4,'col'=16,'rep'=4] {'row'}, dimensions={0} | all-to-all | bytes 16777216 | tf_op jit(solution)/shard_map/all_to_all | solution.py:23
  268.6 0.0 all-gather.2.cloned.1.call-done
  268.6 13.8 %fusion.3 = bf16[1024,2048]{1,0:T(8,128)(2,1)} fusion(bf16[2048,2048]{1,0:T(8,128)(2,1)} %bitcast.25, bf16[1,1024,2048]{2,1,0:T(8,128)(2,1)} %all-gather.2.cloned.1.call-done), kind=kOutput, calls=%fused_computation.5 | convolution fusion | flops 8592031744 | bytes 16777216 | tf_op jit(solution)/shard_map/dot_general | solution.py:26
  282.4 0.0 copy-start.1
  282.5 0.0 reduce-scatter.2.cloned.1.call-update
  282.5 0.7 copy-done.1
  283.1 0.1 copy.6
  283.2 56.9 %reduce-scatter.2.cloned.1.call-done = bf16[1024,512]{1,0:T(8,128)(2,1)} async-done(((bf16[1024,2048]{1,0:T(8,128)(2,1)}), bf16[1024,512]{1,0:T(8,128)(2,1)}) %reduce-scatter.2.cloned.1.call-update) | async-done | bytes 1048592 | tf_op jit(solution)/shard_map/reduce_scatter | solution.py:29
  340.2 0.0 copy-start
  340.2 1.2 broadcast_in_dim.22
  341.4 0.0 copy-done
  341.5 1.4 fusion.7
  (5 shorter events, 0.1 us)
Async XLA Ops:
  6.5 262.1 %all-gather.2.cloned.1.call-start = ((), (), s32[]{:S(2)}) async-start(), calls=%async_computation.2 | async-start | bytes 4456448 | tf_op jit(solution)/shard_map/all_gather | solution.py:18
  138.6 201.5 %reduce-scatter.2.cloned.1.call-start = ((), (), s32[]{:S(2)}) async-start(), calls=%async_computation.3 | async-start | bytes 5242880 | tf_op jit(solution)/shard_map/reduce_scatter | solution.py:29
  282.4 0.7 copy-start.1
  340.2 1.3 copy-start
Sparse Core Ops, SparseCore 0:
  138.7 81.8 all-gather.1
  282.6 57.5 reduce-scatter.1
